TPU v7x, 128 devices: a whole 4x4x4 slice. The times are simulated.
128 devices in a mesh: tm: 8 (over y_hi, z), rows: 16 (over y_lo, x, core).
Axes of the slice: x: 4, y: 4 (y_hi: 2, y_lo: 2; y = y_hi * 2 + y_lo), z: 4, core: 2. Of those that a mesh axis runs over, the one named last changes fastest.
Arguments:
- video: bfloat16 [1, 32, 128, 128, 256], P(None, 'tm', 'rows'), may hold values from -6 to 6
- spatial_weight: bfloat16 [2304, 256], P(('tm', 'rows')), may hold values from -0.125 to 0.125
- temporal_weight: bfloat16 [768, 256], P(('tm', 'rows')), may hold values from -0.21875 to 0.21875
- cotangent: bfloat16 [1, 32, 128, 128, 256], P(None, 'tm', 'rows'), may hold values from -6 to 6
Outputs:
- output: bfloat16 [1, 32, 128, 128, 256], P(None, 'tm', 'rows')
- grad_video: bfloat16 [1, 32, 128, 128, 256], P(None, 'tm', 'rows')
- grad_spatial: float32 [2304, 256], P(('tm', 'rows'))
- grad_temporal: float32 [768, 256], P(('tm', 'rows'))
All inputs are finite; a program needn't handle non-finite values.
Results may differ from a plain program's by a relative error of at most 0.0053.
Values may be sent and summed in bfloat16 or wider, within the bound.
No kernel may reach another device: no remote copies, remote signals or barrier semaphores. Data moves between devices by JAX's collectives and lax.ppermute only.
A program may use at most 128 MiB of HBM per device.

v0:
```python
import jax
import jax.numpy as jnp
from jax import lax
from jax.sharding import PartitionSpec as P

epsilon = 1e-06


def with_halo(x, sides, width):
    for axis, dim in sides:
        count, length = (lax.axis_size(axis), x.shape[dim])
        up = [(i, (i + 1) % count) for i in range(count - 1)]
        down = [(j, i) for i, j in up]
        last = lax.slice_in_dim(x, length - width, length, axis=dim)
        leading = lax.slice_in_dim(x, 0, width, axis=dim)
        before = lax.ppermute(last, axis, up)
        after = lax.ppermute(leading, axis, down)
        x = jnp.concatenate([before, x, after], axis=dim)
    return x


def passed_along(x, axis, by):
    count = lax.axis_size(axis)
    pairs = [(i, i + by) for i in range(count) if 0 <= i + by < count]
    return lax.ppermute(x, axis, pairs)


def rim_pad(field):
    rimmed = with_halo(field, (("rows", 2),), 1)
    return jnp.pad(rimmed, ((0, 0), (0, 0), (0, 0), (1, 1), (0, 0)))


def shifted_view(padded, tap_row, tap_col, n_rows, n_cols):
    chans = padded.shape[-1]
    return padded[:, :, tap_row : tap_row + n_rows, tap_col : tap_col + n_cols].reshape(-1, chans)


def conv_three(padded, weight, n_rows, n_cols):
    chans = padded.shape[-1]
    total = None
    for tap_row in range(3):
        for tap_col in range(3):
            block = weight[(3 * tap_row + tap_col) * chans : (3 * tap_row + tap_col + 1) * chans]
            term = jnp.dot(
                shifted_view(padded, tap_row, tap_col, n_rows, n_cols),
                block,
                preferred_element_type=jnp.float32,
            )
            total = term if total is None else total + term
    return total


def kernel_grad(padded, grad_flat, n_rows, n_cols):
    blocks = [
        contract(shifted_view(padded, tap_row, tap_col, n_rows, n_cols), grad_flat)
        for tap_row in range(3)
        for tap_col in range(3)
    ]
    return jnp.concatenate(blocks, axis=0)


def frame_cols(padded, n_frames):
    chans = padded.shape[-1]
    return jnp.concatenate([padded[:, k : k + n_frames] for k in range(3)], axis=-1).reshape(
        -1, 3 * chans
    )


def silu_slope(value):
    sigmoid = jax.nn.sigmoid(value)
    return sigmoid * (1.0 + value * (1.0 - sigmoid))


def contract(left, right):
    return lax.dot_general(
        left, right, (((0,), (0,)), ((), ())), preferred_element_type=jnp.float32
    )


def reverse_spatial(weight, chans):
    return (
        weight.reshape(3, 3, chans, chans)[::-1, ::-1]
        .transpose(0, 1, 3, 2)
        .reshape(9 * chans, chans)
    )


def reverse_temporal(weight, chans):
    return weight.reshape(3, chans, chans)[::-1].transpose(0, 2, 1).reshape(3 * chans, chans)


def shards(video, spatial_weight, temporal_weight, cotangent):
    n_batch, n_frames, n_rows, n_cols, chans = video.shape
    full_spatial, full_temporal = (
        lax.all_gather(spatial_weight, ("tm", "rows"), axis=0, tiled=True),
        lax.all_gather(temporal_weight, ("tm", "rows"), axis=0, tiled=True),
    )
    values = video.astype(jnp.float32)
    inv_rms = lax.rsqrt(jnp.mean(values * values, axis=-1, keepdims=True) + epsilon)
    normed = values * inv_rms
    activated = jax.nn.silu(normed).astype(jnp.bfloat16)
    padded_act = rim_pad(activated)
    pre_act = conv_three(padded_act, full_spatial, n_rows, n_cols).reshape(video.shape)
    hidden = jax.nn.silu(pre_act).astype(jnp.bfloat16)
    back_temporal = reverse_temporal(full_temporal, chans)
    past = passed_along(hidden[:, n_frames - 2 :], "tm", 1)
    ahead = passed_along(cotangent[:, :2], "tm", -1)
    from_past = frame_cols(jnp.concatenate([past, hidden], axis=1), n_frames)
    from_ahead = frame_cols(jnp.concatenate([cotangent, ahead], axis=1), n_frames)
    mixed = jnp.dot(from_past, full_temporal, preferred_element_type=jnp.float32).reshape(
        video.shape
    )
    back = jnp.dot(from_ahead, back_temporal, preferred_element_type=jnp.float32).reshape(
        video.shape
    )
    grad_temporal = contract(from_past, cotangent.reshape(-1, chans))
    output = (values + mixed).astype(jnp.bfloat16)
    grad_pre = (back * silu_slope(pre_act)).astype(jnp.bfloat16)
    grad_spatial = kernel_grad(padded_act, grad_pre.reshape(-1, chans), n_rows, n_cols)
    back_spatial = reverse_spatial(full_spatial, chans)
    grad_act = conv_three(rim_pad(grad_pre), back_spatial, n_rows, n_cols).reshape(video.shape)
    grad_norm = grad_act * silu_slope(normed)
    grad_in = inv_rms * (grad_norm - normed * jnp.mean(grad_norm * normed, axis=-1, keepdims=True))
    grad_video = (cotangent.astype(jnp.float32) + grad_in).astype(jnp.bfloat16)
    spatial_part, temporal_part = (
        lax.psum_scatter(grad_spatial, ("tm", "rows"), scatter_dimension=0, tiled=True),
        lax.psum_scatter(grad_temporal, ("tm", "rows"), scatter_dimension=0, tiled=True),
    )
    total_cells = n_batch * n_frames * n_rows * n_cols * lax.axis_size("tm") * lax.axis_size("rows")
    factor = float(total_cells) ** (-0.5)
    return (output, grad_video, spatial_part * factor, temporal_part * factor)


def solution(mesh):
    in_specs = (
        P(None, "tm", "rows", None, None),
        P(("tm", "rows"), None),
        P(("tm", "rows"), None),
        P(None, "tm", "rows", None, None),
    )
    out_specs = (
        P(None, "tm", "rows", None, None),
        P(None, "tm", "rows", None, None),
        P(("tm", "rows"), None),
        P(("tm", "rows"), None),
    )
    return jax.shard_map(shards, mesh=mesh, in_specs=in_specs, out_specs=out_specs, check_vma=False)
```

profile of v0, /device:TPU:4, one launch (start us, length us, event | category | flops | bytes accessed | tf_op | source)
XLA Modules:
  0.0 832.9 jit_solution(6420278015430662452)
XLA Ops:
  7.9 2.4 fusion.32
  14.4 3.6 collective-permute-start.1
  20.5 175.8 %all-gather.1 = bf16[128,6,256]{2,1,0:T(8,128)(2,1)S(1)} all-gather(bf16[1,6,256]{2,1,0:T(8,128)(2,1)S(1)} %bitcast.245), channel_id=1, replica_groups=mesh['tm'=8,'rows'=16] {'tm','rows'}, dimensions={0}, use_global_device_ids=true | all-gather | bytes 396288 | tf_op jit(solution)/shard_map/all_gather | solution.py:96
  203.9 5.4 fusion.149
  210.6 2.5 fusion.147
  213.2 8.5 %all-gather.4.cloned.1.call-done = bf16[128,18,256]{2,1,0:T(8,128)(2,1)} async-done(((bf16[1,18,256]{2,1,0:T(8,128)(2,1)}), bf16[128,18,256]{2,1,0:T(8,128)(2,1)}) %all-gather.4.cloned.1.call-update) | async-done | bytes 1179664 | tf_op jit(solution)/shard_map/all_gather | solution.py:95
  221.6 2.3 reshape.272
  224.0 2.4 fusion.135
  236.7 2.7 multiply_convert_fusion.1
  241.6 6.7 collective-permute-start.2
  248.4 3.2 multiply_convert_fusion
  262.8 3.6 collective-permute-start.5
  266.5 3.4 reshape.249
  272.7 3.1 fusion.111
  278.1 3.2 pad_maximum_fusion.1
  281.4 4.6 fusion.148
  285.9 2.8 fusion.124
  291.6 3.8 fusion.57
  295.4 328.1 %fusion.146 = (f32[24,256]{1,0:T(8,128)S(1)}, f32[8,256]{1,0:T(8,128)S(1)}) fusion(f32[2304,256]{1,0:T(8,128)} %fusion.111, f32[768,256]{1,0:T(8,128)} %fusion.57), kind=kCustom, calls=%all-reduce-scatter.2 | all-reduce-scatter fusion | flops 1048578 | bytes 3178496
  630.5 3.7 convolution_add_fusion.6
  640.1 3.7 collective-permute-done.40
  645.9 4.9 collective-permute-done.41
  650.8 10.5 %collective-permute-start.46 = (f32[8,256]{1,0:T(8,128)S(1)}, f32[8,256]{1,0:T(8,128)S(1)}, u32[]{:S(2)}, u32[]{:S(2)}) collective-permute-start(f32[8,256]{1,0:T(8,128)S(1)} %get-tuple-element.7), channel_id=1, source_target_pairs={{0,9},{1,10},{2,11},{3,12},{4,13},{5,14},{6,15},{7,16},{8,17},{9,1... | collective-permute-start | bytes 24584
  661.3 3.1 collective-permute-start.47
  667.4 18.3 %collective-permute-start.50 = (f32[8,256]{1,0:T(8,128)S(1)}, f32[8,256]{1,0:T(8,128)S(1)}, u32[]{:S(2)}, u32[]{:S(2)}) collective-permute-start(f32[8,256]{1,0:T(8,128)S(1)} %get-tuple-element.7), channel_id=1, source_target_pairs={{0,13},{1,14},{2,15},{3,16},{4,17},{5,18},{6,19},{7,20},{8,21},{9,... | collective-permute-start | bytes 24584
  686.5 2.9 collective-permute-start.51
  695.2 3.1 collective-permute-start.55
  699.1 3.8 collective-permute-start.56
  713.9 2.8 collective-permute-start.63
  718.4 2.4 collective-permute-start.65
  725.9 4.0 collective-permute-start.10
  735.9 4.1 collective-permute-start.13
  742.0 3.7 collective-permute-start.15
  748.5 2.9 collective-permute-start.17
  751.4 2.7 collective-permute-start.18
  754.2 3.9 collective-permute-start.19
  759.8 2.4 fusion.27
  764.8 2.6 collective-permute-start.23
  767.4 3.5 collective-permute-start.24
  778.1 2.3 collective-permute-start.29
  782.1 3.7 fusion.31
  785.8 2.8 collective-permute-start.31
  796.0 4.1 fusion.33
  800.3 2.9 concatenate.53
  806.5 2.7 collective-permute-start.7
  809.2 4.5 collective-permute-start.8
  816.3 4.7 collective-permute-done.9
  820.9 4.3 concatenate.52
  (310 shorter events, 127.4 us)
Async XLA Ops:
  7.2 214.5 %all-gather.4.cloned.1.call-start = ((), (), s32[]{:S(2)}) async-start(), calls=%async_computation | async-start | bytes 1585152 | tf_op jit(solution)/shard_map/all_gather | solution.py:95
  12.5 187.5 %collective-permute-start = (bf16[1,4,1,128,256]{4,3,2,1,0:T(8,128)(2,1)}, bf16[1,4,1,128,256]{4,3,2,1,0:T(8,128)(2,1)S(1)}, u32[]{:S(2)}, u32[]{:S(2)}) collective-permute-start(bf16[1,4,1,128,256]{4,3,2,1,0:T(8,128)(2,1)} %get-tuple-element.28), channel_id=1, source_target_pairs={{0,1},{1,2},{2,3},{3,4},{4,5},{5,6},{6,7},{7,8},{8,9},{9,10},{10,1... | collective-permute-start | bytes 786440 | tf_op jit(solution)/shard_map/ppermute | solution.py:16
  14.4 185.5 %collective-permute-start.1 = (bf16[1,4,1,128,256]{4,3,2,1,0:T(8,128)(2,1)}, bf16[1,4,1,128,256]{4,3,2,1,0:T(8,128)(2,1)S(1)}, u32[]{:S(2)}, u32[]{:S(2)}) collective-permute-start(bf16[1,4,1,128,256]{4,3,2,1,0:T(8,128)(2,1)} %get-tuple-element.29), channel_id=1, source_target_pairs={{1,0},{2,1},{3,2},{4,3},{5,4},{6,5},{7,6},{8,7},{9,8},{10,9},{11,1... | collective-permute-start | bytes 786440 | tf_op jit(solution)/shard_map/ppermute | solution.py:17
  19.2 190.2 %collective-permute-start.3 = (bf16[1,2,8,128,256]{4,3,2,1,0:T(8,128)(2,1)}, bf16[1,2,8,128,256]{4,3,2,1,0:T(8,128)(2,1)}, u32[]{:S(2)}, u32[]{:S(2)}) collective-permute-start(bf16[1,2,8,128,256]{4,3,2,1,0:T(8,128)(2,1)} %slice.175), channel_id=1, source_target_pairs={{16,0},{32,16},{48,32},{64,48},{80,64},{96,80},{112,96},{17,1},{33... | collective-permute-start | bytes 3145736 | tf_op jit(solution)/shard_map/ppermute | solution.py:25
  241.6 47.1 %collective-permute-start.2 = (bf16[1,2,8,128,256]{4,3,2,1,0:T(8,128)(2,1)}, bf16[1,2,8,128,256]{4,3,2,1,0:T(8,128)(2,1)}, u32[]{:S(2)}, u32[]{:S(2)}) collective-permute-start(bf16[1,2,8,128,256]{4,3,2,1,0:T(8,128)(2,1)} %slice.214), channel_id=1, source_target_pairs={{0,16},{16,32},{32,48},{48,64},{64,80},{80,96},{96,112},{1,17},{17... | collective-permute-start | bytes 3145736 | tf_op jit(solution)/shard_map/ppermute | solution.py:25
  260.9 14.9 %collective-permute-start.4 = (bf16[1,4,1,128,256]{4,3,2,1,0:T(8,128)(2,1)}, bf16[1,4,1,128,256]{4,3,2,1,0:T(8,128)(2,1)S(1)}, u32[]{:S(2)}, u32[]{:S(2)}) collective-permute-start(bf16[1,4,1,128,256]{4,3,2,1,0:T(8,128)(2,1)} %get-tuple-element.24), channel_id=1, source_target_pairs={{0,1},{1,2},{2,3},{3,4},{4,5},{5,6},{6,7},{7,8},{8,9},{9,10},{10,1... | collective-permute-start | bytes 786440 | tf_op jit(solution)/shard_map/ppermute | solution.py:16
  262.8 13.0 %collective-permute-start.5 = (bf16[1,4,1,128,256]{4,3,2,1,0:T(8,128)(2,1)}, bf16[1,4,1,128,256]{4,3,2,1,0:T(8,128)(2,1)}, u32[]{:S(2)}, u32[]{:S(2)}) collective-permute-start(bf16[1,4,1,128,256]{4,3,2,1,0:T(8,128)(2,1)} %get-tuple-element.25), channel_id=1, source_target_pairs={{1,0},{2,1},{3,2},{4,3},{5,4},{6,5},{7,6},{8,7},{9,8},{10,9},{11,1... | collective-permute-start | bytes 786440 | tf_op jit(solution)/shard_map/ppermute | solution.py:17
  623.4 14.0 %collective-permute-start.38 = (f32[8,256]{1,0:T(8,128)S(1)}, f32[8,256]{1,0:T(8,128)S(1)}, u32[]{:S(2)}, u32[]{:S(2)}) collective-permute-start(f32[8,256]{1,0:T(8,128)S(1)} %get-tuple-element.7), channel_id=1, source_target_pairs={{0,1},{1,2},{2,3},{3,4},{4,5},{5,6},{6,7},{7,8},{8,9},{9,10},{10,1... | collective-permute-start | bytes 24584
  625.4 13.4 %collective-permute-start.39 = (f32[8,256]{1,0:T(8,128)S(1)}, f32[8,256]{1,0:T(8,128)S(1)}, u32[]{:S(2)}, u32[]{:S(2)}) collective-permute-start(f32[8,256]{1,0:T(8,128)S(1)} %get-tuple-element.7), channel_id=1, source_target_pairs={{0,2},{1,3},{2,4},{3,5},{4,6},{5,7},{6,8},{7,9},{8,10},{9,11},{10,... | collective-permute-start | bytes 24584
  627.3 16.5 %collective-permute-start.40 = (f32[8,256]{1,0:T(8,128)S(1)}, f32[8,256]{1,0:T(8,128)S(1)}, u32[]{:S(2)}, u32[]{:S(2)}) collective-permute-start(f32[8,256]{1,0:T(8,128)S(1)} %get-tuple-element.7), channel_id=1, source_target_pairs={{0,3},{1,4},{2,5},{3,6},{4,7},{5,8},{6,9},{7,10},{8,11},{9,12},{10... | collective-permute-start | bytes 24584
  634.2 16.6 %collective-permute-start.41 = (f32[8,256]{1,0:T(8,128)S(1)}, f32[8,256]{1,0:T(8,128)S(1)}, u32[]{:S(2)}, u32[]{:S(2)}) collective-permute-start(f32[8,256]{1,0:T(8,128)S(1)} %get-tuple-element.7), channel_id=1, source_target_pairs={{0,4},{1,5},{2,6},{3,7},{4,8},{5,9},{6,10},{7,11},{8,12},{9,13},{1... | collective-permute-start | bytes 24584
  636.2 25.1 %collective-permute-start.42 = (f32[8,256]{1,0:T(8,128)S(1)}, f32[8,256]{1,0:T(8,128)S(1)}, u32[]{:S(2)}, u32[]{:S(2)}) collective-permute-start(f32[8,256]{1,0:T(8,128)S(1)} %get-tuple-element.7), channel_id=1, source_target_pairs={{0,5},{1,6},{2,7},{3,8},{4,9},{5,10},{6,11},{7,12},{8,13},{9,14},{... | collective-permute-start | bytes 24584
  637.5 26.9 %collective-permute-start.43 = (f32[8,256]{1,0:T(8,128)S(1)}, f32[8,256]{1,0:T(8,128)S(1)}, u32[]{:S(2)}, u32[]{:S(2)}) collective-permute-start(f32[8,256]{1,0:T(8,128)S(1)} %get-tuple-element.7), channel_id=1, source_target_pairs={{0,6},{1,7},{2,8},{3,9},{4,10},{5,11},{6,12},{7,13},{8,14},{9,15},... | collective-permute-start | bytes 24584
  638.8 26.9 %collective-permute-start.44 = (f32[8,256]{1,0:T(8,128)S(1)}, f32[8,256]{1,0:T(8,128)S(1)}, u32[]{:S(2)}, u32[]{:S(2)}) collective-permute-start(f32[8,256]{1,0:T(8,128)S(1)} %get-tuple-element.7), channel_id=1, source_target_pairs={{0,7},{1,8},{2,9},{3,10},{4,11},{5,12},{6,13},{7,14},{8,15},{9,16}... | collective-permute-start | bytes 24584
  643.8 23.5 %collective-permute-start.45 = (f32[8,256]{1,0:T(8,128)S(1)}, f32[8,256]{1,0:T(8,128)S(1)}, u32[]{:S(2)}, u32[]{:S(2)}) collective-permute-start(f32[8,256]{1,0:T(8,128)S(1)} %get-tuple-element.7), channel_id=1, source_target_pairs={{0,8},{1,9},{2,10},{3,11},{4,12},{5,13},{6,14},{7,15},{8,16},{9,17... | collective-permute-start | bytes 24584
  650.8 35.7 %collective-permute-start.46 = (f32[8,256]{1,0:T(8,128)S(1)}, f32[8,256]{1,0:T(8,128)S(1)}, u32[]{:S(2)}, u32[]{:S(2)}) collective-permute-start(f32[8,256]{1,0:T(8,128)S(1)} %get-tuple-element.7), channel_id=1, source_target_pairs={{0,9},{1,10},{2,11},{3,12},{4,13},{5,14},{6,15},{7,16},{8,17},{9,1... | collective-permute-start | bytes 24584
  661.3 28.1 %collective-permute-start.47 = (f32[8,256]{1,0:T(8,128)S(1)}, f32[8,256]{1,0:T(8,128)S(1)}, u32[]{:S(2)}, u32[]{:S(2)}) collective-permute-start(f32[8,256]{1,0:T(8,128)S(1)} %get-tuple-element.7), channel_id=1, source_target_pairs={{0,10},{1,11},{2,12},{3,13},{4,14},{5,15},{6,16},{7,17},{8,18},{9,... | collective-permute-start | bytes 24584
  664.4 27.0 %collective-permute-start.48 = (f32[8,256]{1,0:T(8,128)S(1)}, f32[8,256]{1,0:T(8,128)S(1)}, u32[]{:S(2)}, u32[]{:S(2)}) collective-permute-start(f32[8,256]{1,0:T(8,128)S(1)} %get-tuple-element.7), channel_id=1, source_target_pairs={{0,11},{1,12},{2,13},{3,14},{4,15},{5,16},{6,17},{7,18},{8,19},{9,... | collective-permute-start | bytes 24584
  665.7 27.5 %collective-permute-start.49 = (f32[8,256]{1,0:T(8,128)S(1)}, f32[8,256]{1,0:T(8,128)S(1)}, u32[]{:S(2)}, u32[]{:S(2)}) collective-permute-start(f32[8,256]{1,0:T(8,128)S(1)} %get-tuple-element.7), channel_id=1, source_target_pairs={{0,12},{1,13},{2,14},{3,15},{4,16},{5,17},{6,18},{7,19},{8,20},{9,... | collective-permute-start | bytes 24584
  667.4 27.7 %collective-permute-start.50 = (f32[8,256]{1,0:T(8,128)S(1)}, f32[8,256]{1,0:T(8,128)S(1)}, u32[]{:S(2)}, u32[]{:S(2)}) collective-permute-start(f32[8,256]{1,0:T(8,128)S(1)} %get-tuple-element.7), channel_id=1, source_target_pairs={{0,13},{1,14},{2,15},{3,16},{4,17},{5,18},{6,19},{7,20},{8,21},{9,... | collective-permute-start | bytes 24584
  686.5 12.6 %collective-permute-start.51 = (f32[8,256]{1,0:T(8,128)S(1)}, f32[8,256]{1,0:T(8,128)S(1)}, u32[]{:S(2)}, u32[]{:S(2)}) collective-permute-start(f32[8,256]{1,0:T(8,128)S(1)} %get-tuple-element.7), channel_id=1, source_target_pairs={{0,14},{1,15},{2,16},{3,17},{4,18},{5,19},{6,20},{7,21},{8,22},{9,... | collective-permute-start | bytes 24584
  689.4 13.5 %collective-permute-start.52 = (f32[8,256]{1,0:T(8,128)S(1)}, f32[8,256]{1,0:T(8,128)S(1)}, u32[]{:S(2)}, u32[]{:S(2)}) collective-permute-start(f32[8,256]{1,0:T(8,128)S(1)} %get-tuple-element.7), channel_id=1, source_target_pairs={{0,15},{1,16},{2,17},{3,18},{4,19},{5,20},{6,21},{7,22},{8,23},{9,... | collective-permute-start | bytes 24584
  691.4 13.2 %collective-permute-start.53 = (f32[8,256]{1,0:T(8,128)S(1)}, f32[8,256]{1,0:T(8,128)S(1)}, u32[]{:S(2)}, u32[]{:S(2)}) collective-permute-start(f32[8,256]{1,0:T(8,128)S(1)} %get-tuple-element.7), channel_id=1, source_target_pairs={{0,16},{1,17},{2,18},{3,19},{4,20},{5,21},{6,22},{7,23},{8,24},{9,... | collective-permute-start | bytes 24584
  693.2 13.0 %collective-permute-start.54 = (f32[8,256]{1,0:T(8,128)S(1)}, f32[8,256]{1,0:T(8,128)S(1)}, u32[]{:S(2)}, u32[]{:S(2)}) collective-permute-start(f32[8,256]{1,0:T(8,128)S(1)} %get-tuple-element.7), channel_id=1, source_target_pairs={{0,17},{1,18},{2,19},{3,20},{4,21},{5,22},{6,23},{7,24},{8,25},{9,... | collective-permute-start | bytes 24584
  695.2 12.4 %collective-permute-start.55 = (f32[8,256]{1,0:T(8,128)S(1)}, f32[8,256]{1,0:T(8,128)S(1)}, u32[]{:S(2)}, u32[]{:S(2)}) collective-permute-start(f32[8,256]{1,0:T(8,128)S(1)} %get-tuple-element.7), channel_id=1, source_target_pairs={{0,18},{1,19},{2,20},{3,21},{4,22},{5,23},{6,24},{7,25},{8,26},{9,... | collective-permute-start | bytes 24584
  725.9 16.1 %collective-permute-start.10 = (f32[24,256]{1,0:T(8,128)S(1)}, f32[24,256]{1,0:T(8,128)S(1)}, u32[]{:S(2)}, u32[]{:S(2)}) collective-permute-start(f32[24,256]{1,0:T(8,128)S(1)} %get-tuple-element.6), channel_id=1, source_target_pairs={{0,5},{1,6},{2,7},{3,8},{4,9},{5,10},{6,11},{7,12},{8,13},{9,14},{... | collective-permute-start | bytes 73736
  731.9 14.6 %collective-permute-start.11 = (f32[24,256]{1,0:T(8,128)S(1)}, f32[24,256]{1,0:T(8,128)S(1)}, u32[]{:S(2)}, u32[]{:S(2)}) collective-permute-start(f32[24,256]{1,0:T(8,128)S(1)} %get-tuple-element.6), channel_id=1, source_target_pairs={{0,6},{1,7},{2,8},{3,9},{4,10},{5,11},{6,12},{7,13},{8,14},{9,15},... | collective-permute-start | bytes 73736
  733.7 14.8 %collective-permute-start.12 = (f32[24,256]{1,0:T(8,128)S(1)}, f32[24,256]{1,0:T(8,128)S(1)}, u32[]{:S(2)}, u32[]{:S(2)}) collective-permute-start(f32[24,256]{1,0:T(8,128)S(1)} %get-tuple-element.6), channel_id=1, source_target_pairs={{0,7},{1,8},{2,9},{3,10},{4,11},{5,12},{6,13},{7,14},{8,15},{9,16}... | collective-permute-start | bytes 73736
  735.9 15.5 %collective-permute-start.13 = (f32[24,256]{1,0:T(8,128)S(1)}, f32[24,256]{1,0:T(8,128)S(1)}, u32[]{:S(2)}, u32[]{:S(2)}) collective-permute-start(f32[24,256]{1,0:T(8,128)S(1)} %get-tuple-element.6), channel_id=1, source_target_pairs={{0,8},{1,9},{2,10},{3,11},{4,12},{5,13},{6,14},{7,15},{8,16},{9,17... | collective-permute-start | bytes 73736
  740.0 14.1 %collective-permute-start.14 = (f32[24,256]{1,0:T(8,128)S(1)}, f32[24,256]{1,0:T(8,128)S(1)}, u32[]{:S(2)}, u32[]{:S(2)}) collective-permute-start(f32[24,256]{1,0:T(8,128)S(1)} %get-tuple-element.6), channel_id=1, source_target_pairs={{0,9},{1,10},{2,11},{3,12},{4,13},{5,14},{6,15},{7,16},{8,17},{9,1... | collective-permute-start | bytes 73736
  742.0 16.1 %collective-permute-start.15 = (f32[24,256]{1,0:T(8,128)S(1)}, f32[24,256]{1,0:T(8,128)S(1)}, u32[]{:S(2)}, u32[]{:S(2)}) collective-permute-start(f32[24,256]{1,0:T(8,128)S(1)} %get-tuple-element.6), channel_id=1, source_target_pairs={{0,10},{1,11},{2,12},{3,13},{4,14},{5,15},{6,16},{7,17},{8,18},{9,... | collective-permute-start | bytes 73736
  746.5 15.6 %collective-permute-start.16 = (f32[24,256]{1,0:T(8,128)S(1)}, f32[24,256]{1,0:T(8,128)S(1)}, u32[]{:S(2)}, u32[]{:S(2)}) collective-permute-start(f32[24,256]{1,0:T(8,128)S(1)} %get-tuple-element.6), channel_id=1, source_target_pairs={{0,11},{1,12},{2,13},{3,14},{4,15},{5,16},{6,17},{7,18},{8,19},{9,... | collective-permute-start | bytes 73736
  748.5 14.9 %collective-permute-start.17 = (f32[24,256]{1,0:T(8,128)S(1)}, f32[24,256]{1,0:T(8,128)S(1)}, u32[]{:S(2)}, u32[]{:S(2)}) collective-permute-start(f32[24,256]{1,0:T(8,128)S(1)} %get-tuple-element.6), channel_id=1, source_target_pairs={{0,12},{1,13},{2,14},{3,15},{4,16},{5,17},{6,18},{7,19},{8,20},{9,... | collective-permute-start | bytes 73736
  751.4 13.3 %collective-permute-start.18 = (f32[24,256]{1,0:T(8,128)S(1)}, f32[24,256]{1,0:T(8,128)S(1)}, u32[]{:S(2)}, u32[]{:S(2)}) collective-permute-start(f32[24,256]{1,0:T(8,128)S(1)} %get-tuple-element.6), channel_id=1, source_target_pairs={{0,13},{1,14},{2,15},{3,16},{4,17},{5,18},{6,19},{7,20},{8,21},{9,... | collective-permute-start | bytes 73736
  754.2 13.2 %collective-permute-start.19 = (f32[24,256]{1,0:T(8,128)S(1)}, f32[24,256]{1,0:T(8,128)S(1)}, u32[]{:S(2)}, u32[]{:S(2)}) collective-permute-start(f32[24,256]{1,0:T(8,128)S(1)} %get-tuple-element.6), channel_id=1, source_target_pairs={{0,14},{1,15},{2,16},{3,17},{4,18},{5,19},{6,20},{7,21},{8,22},{9,... | collective-permute-start | bytes 73736
  758.1 12.8 %collective-permute-start.20 = (f32[24,256]{1,0:T(8,128)S(1)}, f32[24,256]{1,0:T(8,128)S(1)}, u32[]{:S(2)}, u32[]{:S(2)}) collective-permute-start(f32[24,256]{1,0:T(8,128)S(1)} %get-tuple-element.6), channel_id=1, source_target_pairs={{0,15},{1,16},{2,17},{3,18},{4,19},{5,20},{6,21},{7,22},{8,23},{9,... | collective-permute-start | bytes 73736
  764.8 11.9 %collective-permute-start.23 = (f32[24,256]{1,0:T(8,128)S(1)}, f32[24,256]{1,0:T(8,128)S(1)}, u32[]{:S(2)}, u32[]{:S(2)}) collective-permute-start(f32[24,256]{1,0:T(8,128)S(1)} %get-tuple-element.6), channel_id=1, source_target_pairs={{0,18},{1,19},{2,20},{3,21},{4,22},{5,23},{6,24},{7,25},{8,26},{9,... | collective-permute-start | bytes 73736
  772.7 13.1 %collective-permute-start.26 = (f32[24,256]{1,0:T(8,128)S(1)}, f32[24,256]{1,0:T(8,128)S(1)}, u32[]{:S(2)}, u32[]{:S(2)}) collective-permute-start(f32[24,256]{1,0:T(8,128)S(1)} %get-tuple-element.6), channel_id=1, source_target_pairs={{0,21},{1,22},{2,23},{3,24},{4,25},{5,26},{6,27},{7,28},{8,29},{9,... | collective-permute-start | bytes 73736
  774.6 13.9 %collective-permute-start.27 = (f32[24,256]{1,0:T(8,128)S(1)}, f32[24,256]{1,0:T(8,128)S(1)}, u32[]{:S(2)}, u32[]{:S(2)}) collective-permute-start(f32[24,256]{1,0:T(8,128)S(1)} %get-tuple-element.6), channel_id=1, source_target_pairs={{0,22},{1,23},{2,24},{3,25},{4,26},{5,27},{6,28},{7,29},{8,30},{9,... | collective-permute-start | bytes 73736
  776.7 13.6 %collective-permute-start.28 = (f32[24,256]{1,0:T(8,128)S(1)}, f32[24,256]{1,0:T(8,128)S(1)}, u32[]{:S(2)}, u32[]{:S(2)}) collective-permute-start(f32[24,256]{1,0:T(8,128)S(1)} %get-tuple-element.6), channel_id=1, source_target_pairs={{0,23},{1,24},{2,25},{3,26},{4,27},{5,28},{6,29},{7,30},{8,31},{9,... | collective-permute-start | bytes 73736
  778.1 14.2 %collective-permute-start.29 = (f32[24,256]{1,0:T(8,128)S(1)}, f32[24,256]{1,0:T(8,128)S(1)}, u32[]{:S(2)}, u32[]{:S(2)}) collective-permute-start(f32[24,256]{1,0:T(8,128)S(1)} %get-tuple-element.6), channel_id=1, source_target_pairs={{0,24},{1,25},{2,26},{3,27},{4,28},{5,29},{6,30},{7,31},{8,32},{9,... | collective-permute-start | bytes 73736
  780.4 13.1 %collective-permute-start.30 = (f32[24,256]{1,0:T(8,128)S(1)}, f32[24,256]{1,0:T(8,128)S(1)}, u32[]{:S(2)}, u32[]{:S(2)}) collective-permute-start(f32[24,256]{1,0:T(8,128)S(1)} %get-tuple-element.6), channel_id=1, source_target_pairs={{0,25},{1,26},{2,27},{3,28},{4,29},{5,30},{6,31},{7,32},{8,33},{9,... | collective-permute-start | bytes 73736
  785.8 17.4 %collective-permute-start.31 = (f32[24,256]{1,0:T(8,128)S(1)}, f32[24,256]{1,0:T(8,128)S(1)}, u32[]{:S(2)}, u32[]{:S(2)}) collective-permute-start(f32[24,256]{1,0:T(8,128)S(1)} %get-tuple-element.6), channel_id=1, source_target_pairs={{0,26},{1,27},{2,28},{3,29},{4,30},{5,31},{6,32},{7,33},{8,34},{9,... | collective-permute-start | bytes 73736
  788.6 15.9 %collective-permute-start.32 = (f32[24,256]{1,0:T(8,128)S(1)}, f32[24,256]{1,0:T(8,128)S(1)}, u32[]{:S(2)}, u32[]{:S(2)}) collective-permute-start(f32[24,256]{1,0:T(8,128)S(1)} %get-tuple-element.6), channel_id=1, source_target_pairs={{0,27},{1,28},{2,29},{3,30},{4,31},{5,32},{6,33},{7,34},{8,35},{9,... | collective-permute-start | bytes 73736
  790.2 16.2 %collective-permute-start.33 = (f32[24,256]{1,0:T(8,128)S(1)}, f32[24,256]{1,0:T(8,128)S(1)}, u32[]{:S(2)}, u32[]{:S(2)}) collective-permute-start(f32[24,256]{1,0:T(8,128)S(1)} %get-tuple-element.6), channel_id=1, source_target_pairs={{0,28},{1,29},{2,30},{3,31},{4,32},{5,33},{6,34},{7,35},{8,36},{9,... | collective-permute-start | bytes 73736
  792.2 17.0 %collective-permute-start.34 = (f32[24,256]{1,0:T(8,128)S(1)}, f32[24,256]{1,0:T(8,128)S(1)}, u32[]{:S(2)}, u32[]{:S(2)}) collective-permute-start(f32[24,256]{1,0:T(8,128)S(1)} %get-tuple-element.6), channel_id=1, source_target_pairs={{0,29},{1,30},{2,31},{3,32},{4,33},{5,34},{6,35},{7,36},{8,37},{9,... | collective-permute-start | bytes 73736
  793.6 20.1 %collective-permute-start.35 = (f32[24,256]{1,0:T(8,128)S(1)}, f32[24,256]{1,0:T(8,128)S(1)}, u32[]{:S(2)}, u32[]{:S(2)}) collective-permute-start(f32[24,256]{1,0:T(8,128)S(1)} %get-tuple-element.6), channel_id=1, source_target_pairs={{0,30},{1,31},{2,32},{3,33},{4,34},{5,35},{6,36},{7,37},{8,38},{9,... | collective-permute-start | bytes 73736
  803.2 13.0 %collective-permute-start.36 = (f32[24,256]{1,0:T(8,128)S(1)}, f32[24,256]{1,0:T(8,128)S(1)}, u32[]{:S(2)}, u32[]{:S(2)}) collective-permute-start(f32[24,256]{1,0:T(8,128)S(1)} %get-tuple-element.6), channel_id=1, source_target_pairs={{0,31},{1,32},{2,33},{3,34},{4,35},{5,36},{6,37},{7,38},{8,39},{9,... | collective-permute-start | bytes 73736
  (97 other events, 1081.3 us)
Sparse Core Ops, SparseCore 0:
  9.7 211.8 all-gather.3
where the time goes:
time: 839 us; the launch traced here: 833 us
  blocking collectives  504 us (60%)
  starting transfers between devices  179 us (21%)
  local copies, waits for them, and re-layouts  46.3 us (6%)
  matrix products  41.9 us (5%)
  other arithmetic  23.1 us (3%)
  waiting for transfers between devices  22.6 us (3%)
  between operations  16.5 us (2%)
    unnamed x1, blocking collectives  328 us
    all_gather x1, blocking collectives, shards(): lax.all_gather(temporal_weight, ('tm', 'rows'), axis=0, tiled=True)  176 us
    unnamed x64, starting transfers between devices  160 us
    dot_general x18, matrix products, conv_three(): jnp.dot(shifted_view(padded, tap_row, tap_col, n_rows, n_cols), block, pr...  21.6 us
    unnamed x155, local copies, waits for them, and re-layouts  21.2 us
  transfers between devices with their start and end apart: 71, of which 4 were waited for; matrix products, arithmetic and copies ran while one was open for 9% of the time, Pallas kernels for 0%

commit v1 on v0

--- a/solution.py
+++ b/solution.py
@@ -4,6 +4,13 @@
 from jax.sharding import PartitionSpec as P
 
 epsilon = 1e-06
+
+
+def exchange_gather(array, axis, dim):
+    size = lax.axis_size(axis)
+    pieces = jnp.stack([array for _ in range(size)])
+    pieces = lax.all_to_all(pieces, axis, split_axis=0, concat_axis=0)
+    return jnp.concatenate(pieces, axis=dim)
 
 
 def with_halo(x, sides, width):
@@ -93,7 +100,7 @@
     n_batch, n_frames, n_rows, n_cols, chans = video.shape
     full_spatial, full_temporal = (
         lax.all_gather(spatial_weight, ("tm", "rows"), axis=0, tiled=True),
-        lax.all_gather(temporal_weight, ("tm", "rows"), axis=0, tiled=True),
+        exchange_gather(temporal_weight, ("tm", "rows"), 0),
     )
     values = video.astype(jnp.float32)
     inv_rms = lax.rsqrt(jnp.mean(values * values, axis=-1, keepdims=True) + epsilon)

time: 839 us -> 839 us (level)
  blocking collectives: 504 us -> 322 us
  waiting for transfers between devices: 22.6 us -> 178 us
  starting transfers between devices: 179 us -> 202 us
    all_gather x1 -> x0, blocking collectives: 176 us -> none  [shards(): lax.all_gather(temporal_weight, ('tm', 'rows'), axis=0, tiled=True)]
    all_gather x1, waiting for transfers between devices: 8.46 us -> 154 us  [shards(): lax.all_gather(spatial_weight, ('tm', 'rows'), axis=0, tiled=True)]
    all_to_all x0 -> x1, starting transfers between devices: none -> 13 us  [exchange_gather(): pieces = lax.all_to_all(pieces, axis, split_axis=0, concat_axis=0)]
    all_to_all x0 -> x1, waiting for transfers between devices: none -> 10.6 us  [exchange_gather(): pieces = lax.all_to_all(pieces, axis, split_axis=0, concat_axis=0)]
    ppermute x2, starting transfers between devices: 7.99 us -> 17.6 us  [passed_along(): return lax.ppermute(x, axis, pairs)]
    unnamed x155 -> x154, local copies, waits for them, and re-layouts: 21.2 us -> 21.7 us
  transfers between devices with their start and end apart: 71 -> 72, of which waited for: 4 -> 5; matrix products, arithmetic and copies ran while one was open for 9% -> 10% of each run, Pallas kernels for 0% -> 0%
where the time goes in v1:
time: 839 us; the launch traced here: 833 us
  blocking collectives  322 us (38%)
  starting transfers between devices  202 us (24%)
  waiting for transfers between devices  178 us (21%)
  local copies, waits for them, and re-layouts  51.6 us (6%)
  matrix products  41.3 us (5%)
  other arithmetic  22.8 us (3%)
  between operations  16.5 us (2%)
    unnamed x1, blocking collectives  322 us
    unnamed x64, starting transfers between devices  160 us
    all_gather x1, waiting for transfers between devices, shards(): lax.all_gather(spatial_weight, ('tm', 'rows'), axis=0, tiled=True)  154 us
    unnamed x154, local copies, waits for them, and re-layouts  21.7 us
    dot_general x18, matrix products, conv_three(): jnp.dot(shifted_view(padded, tap_row, tap_col, n_rows, n_cols), block, pr...  21.6 us
    ppermute x2, starting transfers between devices, passed_along(): return lax.ppermute(x, axis, pairs)  17.6 us
  transfers between devices with their start and end apart: 72, of which 5 were waited for; matrix products, arithmetic and copies ran while one was open for 10% of the time, Pallas kernels for 0%

profile of v1, /device:TPU:4, one launch (start us, length us, event | category | flops | bytes accessed | tf_op | source)
XLA Modules:
  0.0 833.3 jit_solution(12150884721047331720)
XLA Ops:
  7.9 2.4 fusion.32
  14.3 3.6 collective-permute-start.1
  21.2 13.0 %all-to-all-start = ((bf16[128,6,256]{2,1,0:T(8,128)(2,1)}), bf16[128,6,256]{2,1,0:T(8,128)(2,1)S(1)}, u32[]{:S(2)}, u32[]{:S(2)}) async-start(bf16[128,6,256]{2,1,0:T(8,128)(2,1)} %stack.2), calls=%async_computation | async-start | bytes 1048576 | tf_op jit(solution)/shard_map/all_to_all | solution.py:12
  34.2 3.1 constant_dynamic-update-slice_fusion.1
  38.7 5.4 fusion.149
  46.4 10.6 %all-to-all-done = bf16[128,6,256]{2,1,0:T(8,128)(2,1)S(1)} async-done(((bf16[128,6,256]{2,1,0:T(8,128)(2,1)}), bf16[128,6,256]{2,1,0:T(8,128)(2,1)S(1)}, u32[]{:S(2)}, u32[]{:S(2)}) %all-to-all-start) | async-done | bytes 393248 | tf_op jit(solution)/shard_map/all_to_all | solution.py:12
  61.3 4.9 fusion.147
  66.2 153.5 %all-gather.3.cloned.1.call-done = bf16[128,18,256]{2,1,0:T(8,128)(2,1)} async-done(((bf16[1,18,256]{2,1,0:T(8,128)(2,1)}), bf16[128,18,256]{2,1,0:T(8,128)(2,1)}) %all-gather.3.cloned.1.call-update) | async-done | bytes 1179664 | tf_op jit(solution)/shard_map/all_gather | solution.py:102
  222.0 2.4 fusion.135
  234.8 2.7 multiply_convert_fusion.1
  239.7 16.3 %collective-permute-start.2 = (bf16[1,2,8,128,256]{4,3,2,1,0:T(8,128)(2,1)}, bf16[1,2,8,128,256]{4,3,2,1,0:T(8,128)(2,1)}, u32[]{:S(2)}, u32[]{:S(2)}) collective-permute-start(bf16[1,2,8,128,256]{4,3,2,1,0:T(8,128)(2,1)} %slice.214), channel_id=1, source_target_pairs={{0,16},{16,32},{32,48},{48,64},{64,80},{80,96},{96,112},{1,17},{17... | collective-permute-start | bytes 3145736 | tf_op jit(solution)/shard_map/ppermute | solution.py:32
  256.1 2.7 multiply_convert_fusion
  270.0 3.6 collective-permute-start.5
  273.6 3.2 reshape.251
  279.7 3.1 fusion.111
  285.1 3.2 pad_maximum_fusion.1
  288.3 4.6 fusion.148
  292.9 2.7 fusion.124
  298.5 3.8 fusion.57
  302.3 321.5 %fusion.146 = (f32[24,256]{1,0:T(8,128)S(1)}, f32[8,256]{1,0:T(8,128)S(1)}) fusion(f32[2304,256]{1,0:T(8,128)} %fusion.111, f32[768,256]{1,0:T(8,128)} %fusion.57), kind=kCustom, calls=%all-reduce-scatter.2 | all-reduce-scatter fusion | flops 1048578 | bytes 3178496
  630.9 3.7 convolution_add_fusion.6
  642.9 8.1 collective-permute-done.41
  651.0 10.5 %collective-permute-start.46 = (f32[8,256]{1,0:T(8,128)S(1)}, f32[8,256]{1,0:T(8,128)S(1)}, u32[]{:S(2)}, u32[]{:S(2)}) collective-permute-start(f32[8,256]{1,0:T(8,128)S(1)} %get-tuple-element.7), channel_id=1, source_target_pairs={{0,9},{1,10},{2,11},{3,12},{4,13},{5,14},{6,15},{7,16},{8,17},{9,1... | collective-permute-start | bytes 24584
  661.5 3.1 collective-permute-start.47
  667.6 18.5 %collective-permute-start.50 = (f32[8,256]{1,0:T(8,128)S(1)}, f32[8,256]{1,0:T(8,128)S(1)}, u32[]{:S(2)}, u32[]{:S(2)}) collective-permute-start(f32[8,256]{1,0:T(8,128)S(1)} %get-tuple-element.7), channel_id=1, source_target_pairs={{0,13},{1,14},{2,15},{3,16},{4,17},{5,18},{6,19},{7,20},{8,21},{9,... | collective-permute-start | bytes 24584
  686.9 2.9 collective-permute-start.51
  695.5 3.1 collective-permute-start.55
  699.5 3.8 collective-permute-start.56
  714.3 2.8 collective-permute-start.63
  718.8 2.4 collective-permute-start.65
  726.3 4.0 collective-permute-start.10
  736.2 4.2 collective-permute-start.13
  742.4 3.7 collective-permute-start.15
  748.9 2.9 collective-permute-start.17
  751.8 2.7 collective-permute-start.18
  754.6 3.9 collective-permute-start.19
  760.1 2.4 fusion.27
  765.1 2.6 collective-permute-start.23
  767.8 3.5 collective-permute-start.24
  778.5 2.3 collective-permute-start.29
  782.5 3.7 fusion.31
  786.2 2.8 collective-permute-start.31
  796.4 4.1 fusion.33
  800.7 2.9 concatenate.53
  806.9 2.7 collective-permute-start.7
  809.6 4.5 collective-permute-start.8
  816.7 4.7 collective-permute-done.9
  821.3 4.3 concatenate.52
  (312 shorter events, 129.8 us)
Async XLA Ops:
  7.2 212.5 %all-gather.3.cloned.1.call-start = ((), (), s32[]{:S(2)}) async-start(), calls=%async_computation.1 | async-start | bytes 1585152 | tf_op jit(solution)/shard_map/all_gather | solution.py:102
  12.4 25.0 %collective-permute-start = (bf16[1,4,1,128,256]{4,3,2,1,0:T(8,128)(2,1)}, bf16[1,4,1,128,256]{4,3,2,1,0:T(8,128)(2,1)S(1)}, u32[]{:S(2)}, u32[]{:S(2)}) collective-permute-start(bf16[1,4,1,128,256]{4,3,2,1,0:T(8,128)(2,1)} %get-tuple-element.28), channel_id=1, source_target_pairs={{0,1},{1,2},{2,3},{3,4},{4,5},{5,6},{6,7},{7,8},{8,9},{9,10},{10,1... | collective-permute-start | bytes 786440 | tf_op jit(solution)/shard_map/ppermute | solution.py:23
  14.3 23.1 %collective-permute-start.1 = (bf16[1,4,1,128,256]{4,3,2,1,0:T(8,128)(2,1)S(1)}, bf16[1,4,1,128,256]{4,3,2,1,0:T(8,128)(2,1)S(1)}, u32[]{:S(2)}, u32[]{:S(2)}) collective-permute-start(bf16[1,4,1,128,256]{4,3,2,1,0:T(8,128)(2,1)S(1)} %get-tuple-element.29), channel_id=1, source_target_pairs={{1,0},{2,1},{3,2},{4,3},{5,4},{6,5},{7,6},{8,7},{9,8},{10,9},{11,1... | collective-permute-start | bytes 786440 | tf_op jit(solution)/shard_map/ppermute | solution.py:24
  19.1 39.9 %collective-permute-start.3 = (bf16[1,2,8,128,256]{4,3,2,1,0:T(8,128)(2,1)}, bf16[1,2,8,128,256]{4,3,2,1,0:T(8,128)(2,1)}, u32[]{:S(2)}, u32[]{:S(2)}) collective-permute-start(bf16[1,2,8,128,256]{4,3,2,1,0:T(8,128)(2,1)} %slice.175), channel_id=1, source_target_pairs={{16,0},{32,16},{48,32},{64,48},{80,64},{96,80},{112,96},{17,1},{33... | collective-permute-start | bytes 3145736 | tf_op jit(solution)/shard_map/ppermute | solution.py:32
  21.2 35.8 %all-to-all-start = ((bf16[128,6,256]{2,1,0:T(8,128)(2,1)}), bf16[128,6,256]{2,1,0:T(8,128)(2,1)S(1)}, u32[]{:S(2)}, u32[]{:S(2)}) async-start(bf16[128,6,256]{2,1,0:T(8,128)(2,1)} %stack.2), calls=%async_computation | async-start | bytes 1048576 | tf_op jit(solution)/shard_map/all_to_all | solution.py:12
  239.7 55.9 %collective-permute-start.2 = (bf16[1,2,8,128,256]{4,3,2,1,0:T(8,128)(2,1)}, bf16[1,2,8,128,256]{4,3,2,1,0:T(8,128)(2,1)}, u32[]{:S(2)}, u32[]{:S(2)}) collective-permute-start(bf16[1,2,8,128,256]{4,3,2,1,0:T(8,128)(2,1)} %slice.214), channel_id=1, source_target_pairs={{0,16},{16,32},{32,48},{48,64},{64,80},{80,96},{96,112},{1,17},{17... | collective-permute-start | bytes 3145736 | tf_op jit(solution)/shard_map/ppermute | solution.py:32
  268.0 14.7 %collective-permute-start.4 = (bf16[1,4,1,128,256]{4,3,2,1,0:T(8,128)(2,1)}, bf16[1,4,1,128,256]{4,3,2,1,0:T(8,128)(2,1)S(1)}, u32[]{:S(2)}, u32[]{:S(2)}) collective-permute-start(bf16[1,4,1,128,256]{4,3,2,1,0:T(8,128)(2,1)} %get-tuple-element.24), channel_id=1, source_target_pairs={{0,1},{1,2},{2,3},{3,4},{4,5},{5,6},{6,7},{7,8},{8,9},{9,10},{10,1... | collective-permute-start | bytes 786440 | tf_op jit(solution)/shard_map/ppermute | solution.py:23
  270.0 12.8 %collective-permute-start.5 = (bf16[1,4,1,128,256]{4,3,2,1,0:T(8,128)(2,1)}, bf16[1,4,1,128,256]{4,3,2,1,0:T(8,128)(2,1)}, u32[]{:S(2)}, u32[]{:S(2)}) collective-permute-start(bf16[1,4,1,128,256]{4,3,2,1,0:T(8,128)(2,1)} %get-tuple-element.25), channel_id=1, source_target_pairs={{1,0},{2,1},{3,2},{4,3},{5,4},{6,5},{7,6},{8,7},{9,8},{10,9},{11,1... | collective-permute-start | bytes 786440 | tf_op jit(solution)/shard_map/ppermute | solution.py:24
  623.8 14.0 %collective-permute-start.38 = (f32[8,256]{1,0:T(8,128)S(1)}, f32[8,256]{1,0:T(8,128)S(1)}, u32[]{:S(2)}, u32[]{:S(2)}) collective-permute-start(f32[8,256]{1,0:T(8,128)S(1)} %get-tuple-element.7), channel_id=1, source_target_pairs={{0,1},{1,2},{2,3},{3,4},{4,5},{5,6},{6,7},{7,8},{8,9},{9,10},{10,1... | collective-permute-start | bytes 24584
  625.8 13.4 %collective-permute-start.39 = (f32[8,256]{1,0:T(8,128)S(1)}, f32[8,256]{1,0:T(8,128)S(1)}, u32[]{:S(2)}, u32[]{:S(2)}) collective-permute-start(f32[8,256]{1,0:T(8,128)S(1)} %get-tuple-element.7), channel_id=1, source_target_pairs={{0,2},{1,3},{2,4},{3,5},{4,6},{5,7},{6,8},{7,9},{8,10},{9,11},{10,... | collective-permute-start | bytes 24584
  627.7 13.1 %collective-permute-start.40 = (f32[8,256]{1,0:T(8,128)S(1)}, f32[8,256]{1,0:T(8,128)S(1)}, u32[]{:S(2)}, u32[]{:S(2)}) collective-permute-start(f32[8,256]{1,0:T(8,128)S(1)} %get-tuple-element.7), channel_id=1, source_target_pairs={{0,3},{1,4},{2,5},{3,6},{4,7},{5,8},{6,9},{7,10},{8,11},{9,12},{10... | collective-permute-start | bytes 24584
  634.6 16.4 %collective-permute-start.41 = (f32[8,256]{1,0:T(8,128)S(1)}, f32[8,256]{1,0:T(8,128)S(1)}, u32[]{:S(2)}, u32[]{:S(2)}) collective-permute-start(f32[8,256]{1,0:T(8,128)S(1)} %get-tuple-element.7), channel_id=1, source_target_pairs={{0,4},{1,5},{2,6},{3,7},{4,8},{5,9},{6,10},{7,11},{8,12},{9,13},{1... | collective-permute-start | bytes 24584
  636.6 24.9 %collective-permute-start.42 = (f32[8,256]{1,0:T(8,128)S(1)}, f32[8,256]{1,0:T(8,128)S(1)}, u32[]{:S(2)}, u32[]{:S(2)}) collective-permute-start(f32[8,256]{1,0:T(8,128)S(1)} %get-tuple-element.7), channel_id=1, source_target_pairs={{0,5},{1,6},{2,7},{3,8},{4,9},{5,10},{6,11},{7,12},{8,13},{9,14},{... | collective-permute-start | bytes 24584
  637.9 26.7 %collective-permute-start.43 = (f32[8,256]{1,0:T(8,128)S(1)}, f32[8,256]{1,0:T(8,128)S(1)}, u32[]{:S(2)}, u32[]{:S(2)}) collective-permute-start(f32[8,256]{1,0:T(8,128)S(1)} %get-tuple-element.7), channel_id=1, source_target_pairs={{0,6},{1,7},{2,8},{3,9},{4,10},{5,11},{6,12},{7,13},{8,14},{9,15},... | collective-permute-start | bytes 24584
  639.2 26.7 %collective-permute-start.44 = (f32[8,256]{1,0:T(8,128)S(1)}, f32[8,256]{1,0:T(8,128)S(1)}, u32[]{:S(2)}, u32[]{:S(2)}) collective-permute-start(f32[8,256]{1,0:T(8,128)S(1)} %get-tuple-element.7), channel_id=1, source_target_pairs={{0,7},{1,8},{2,9},{3,10},{4,11},{5,12},{6,13},{7,14},{8,15},{9,16}... | collective-permute-start | bytes 24584
  640.8 26.7 %collective-permute-start.45 = (f32[8,256]{1,0:T(8,128)S(1)}, f32[8,256]{1,0:T(8,128)S(1)}, u32[]{:S(2)}, u32[]{:S(2)}) collective-permute-start(f32[8,256]{1,0:T(8,128)S(1)} %get-tuple-element.7), channel_id=1, source_target_pairs={{0,8},{1,9},{2,10},{3,11},{4,12},{5,13},{6,14},{7,15},{8,16},{9,17... | collective-permute-start | bytes 24584
  651.0 35.9 %collective-permute-start.46 = (f32[8,256]{1,0:T(8,128)S(1)}, f32[8,256]{1,0:T(8,128)S(1)}, u32[]{:S(2)}, u32[]{:S(2)}) collective-permute-start(f32[8,256]{1,0:T(8,128)S(1)} %get-tuple-element.7), channel_id=1, source_target_pairs={{0,9},{1,10},{2,11},{3,12},{4,13},{5,14},{6,15},{7,16},{8,17},{9,1... | collective-permute-start | bytes 24584
  661.5 28.3 %collective-permute-start.47 = (f32[8,256]{1,0:T(8,128)S(1)}, f32[8,256]{1,0:T(8,128)S(1)}, u32[]{:S(2)}, u32[]{:S(2)}) collective-permute-start(f32[8,256]{1,0:T(8,128)S(1)} %get-tuple-element.7), channel_id=1, source_target_pairs={{0,10},{1,11},{2,12},{3,13},{4,14},{5,15},{6,16},{7,17},{8,18},{9,... | collective-permute-start | bytes 24584
  664.6 27.2 %collective-permute-start.48 = (f32[8,256]{1,0:T(8,128)S(1)}, f32[8,256]{1,0:T(8,128)S(1)}, u32[]{:S(2)}, u32[]{:S(2)}) collective-permute-start(f32[8,256]{1,0:T(8,128)S(1)} %get-tuple-element.7), channel_id=1, source_target_pairs={{0,11},{1,12},{2,13},{3,14},{4,15},{5,16},{6,17},{7,18},{8,19},{9,... | collective-permute-start | bytes 24584
  665.9 27.7 %collective-permute-start.49 = (f32[8,256]{1,0:T(8,128)S(1)}, f32[8,256]{1,0:T(8,128)S(1)}, u32[]{:S(2)}, u32[]{:S(2)}) collective-permute-start(f32[8,256]{1,0:T(8,128)S(1)} %get-tuple-element.7), channel_id=1, source_target_pairs={{0,12},{1,13},{2,14},{3,15},{4,16},{5,17},{6,18},{7,19},{8,20},{9,... | collective-permute-start | bytes 24584
  667.6 27.9 %collective-permute-start.50 = (f32[8,256]{1,0:T(8,128)S(1)}, f32[8,256]{1,0:T(8,128)S(1)}, u32[]{:S(2)}, u32[]{:S(2)}) collective-permute-start(f32[8,256]{1,0:T(8,128)S(1)} %get-tuple-element.7), channel_id=1, source_target_pairs={{0,13},{1,14},{2,15},{3,16},{4,17},{5,18},{6,19},{7,20},{8,21},{9,... | collective-permute-start | bytes 24584
  686.9 12.6 %collective-permute-start.51 = (f32[8,256]{1,0:T(8,128)S(1)}, f32[8,256]{1,0:T(8,128)S(1)}, u32[]{:S(2)}, u32[]{:S(2)}) collective-permute-start(f32[8,256]{1,0:T(8,128)S(1)} %get-tuple-element.7), channel_id=1, source_target_pairs={{0,14},{1,15},{2,16},{3,17},{4,18},{5,19},{6,20},{7,21},{8,22},{9,... | collective-permute-start | bytes 24584
  689.8 13.5 %collective-permute-start.52 = (f32[8,256]{1,0:T(8,128)S(1)}, f32[8,256]{1,0:T(8,128)S(1)}, u32[]{:S(2)}, u32[]{:S(2)}) collective-permute-start(f32[8,256]{1,0:T(8,128)S(1)} %get-tuple-element.7), channel_id=1, source_target_pairs={{0,15},{1,16},{2,17},{3,18},{4,19},{5,20},{6,21},{7,22},{8,23},{9,... | collective-permute-start | bytes 24584
  691.8 13.2 %collective-permute-start.53 = (f32[8,256]{1,0:T(8,128)S(1)}, f32[8,256]{1,0:T(8,128)S(1)}, u32[]{:S(2)}, u32[]{:S(2)}) collective-permute-start(f32[8,256]{1,0:T(8,128)S(1)} %get-tuple-element.7), channel_id=1, source_target_pairs={{0,16},{1,17},{2,18},{3,19},{4,20},{5,21},{6,22},{7,23},{8,24},{9,... | collective-permute-start | bytes 24584
  693.6 13.0 %collective-permute-start.54 = (f32[8,256]{1,0:T(8,128)S(1)}, f32[8,256]{1,0:T(8,128)S(1)}, u32[]{:S(2)}, u32[]{:S(2)}) collective-permute-start(f32[8,256]{1,0:T(8,128)S(1)} %get-tuple-element.7), channel_id=1, source_target_pairs={{0,17},{1,18},{2,19},{3,20},{4,21},{5,22},{6,23},{7,24},{8,25},{9,... | collective-permute-start | bytes 24584
  695.5 12.4 %collective-permute-start.55 = (f32[8,256]{1,0:T(8,128)S(1)}, f32[8,256]{1,0:T(8,128)S(1)}, u32[]{:S(2)}, u32[]{:S(2)}) collective-permute-start(f32[8,256]{1,0:T(8,128)S(1)} %get-tuple-element.7), channel_id=1, source_target_pairs={{0,18},{1,19},{2,20},{3,21},{4,22},{5,23},{6,24},{7,25},{8,26},{9,... | collective-permute-start | bytes 24584
  726.3 16.1 %collective-permute-start.10 = (f32[24,256]{1,0:T(8,128)S(1)}, f32[24,256]{1,0:T(8,128)S(1)}, u32[]{:S(2)}, u32[]{:S(2)}) collective-permute-start(f32[24,256]{1,0:T(8,128)S(1)} %get-tuple-element.6), channel_id=1, source_target_pairs={{0,5},{1,6},{2,7},{3,8},{4,9},{5,10},{6,11},{7,12},{8,13},{9,14},{... | collective-permute-start | bytes 73736
  732.3 14.6 %collective-permute-start.11 = (f32[24,256]{1,0:T(8,128)S(1)}, f32[24,256]{1,0:T(8,128)S(1)}, u32[]{:S(2)}, u32[]{:S(2)}) collective-permute-start(f32[24,256]{1,0:T(8,128)S(1)} %get-tuple-element.6), channel_id=1, source_target_pairs={{0,6},{1,7},{2,8},{3,9},{4,10},{5,11},{6,12},{7,13},{8,14},{9,15},... | collective-permute-start | bytes 73736
  734.1 14.8 %collective-permute-start.12 = (f32[24,256]{1,0:T(8,128)S(1)}, f32[24,256]{1,0:T(8,128)S(1)}, u32[]{:S(2)}, u32[]{:S(2)}) collective-permute-start(f32[24,256]{1,0:T(8,128)S(1)} %get-tuple-element.6), channel_id=1, source_target_pairs={{0,7},{1,8},{2,9},{3,10},{4,11},{5,12},{6,13},{7,14},{8,15},{9,16}... | collective-permute-start | bytes 73736
  736.2 15.6 %collective-permute-start.13 = (f32[24,256]{1,0:T(8,128)S(1)}, f32[24,256]{1,0:T(8,128)S(1)}, u32[]{:S(2)}, u32[]{:S(2)}) collective-permute-start(f32[24,256]{1,0:T(8,128)S(1)} %get-tuple-element.6), channel_id=1, source_target_pairs={{0,8},{1,9},{2,10},{3,11},{4,12},{5,13},{6,14},{7,15},{8,16},{9,17... | collective-permute-start | bytes 73736
  740.4 14.1 %collective-permute-start.14 = (f32[24,256]{1,0:T(8,128)S(1)}, f32[24,256]{1,0:T(8,128)S(1)}, u32[]{:S(2)}, u32[]{:S(2)}) collective-permute-start(f32[24,256]{1,0:T(8,128)S(1)} %get-tuple-element.6), channel_id=1, source_target_pairs={{0,9},{1,10},{2,11},{3,12},{4,13},{5,14},{6,15},{7,16},{8,17},{9,1... | collective-permute-start | bytes 73736
  742.4 16.1 %collective-permute-start.15 = (f32[24,256]{1,0:T(8,128)S(1)}, f32[24,256]{1,0:T(8,128)S(1)}, u32[]{:S(2)}, u32[]{:S(2)}) collective-permute-start(f32[24,256]{1,0:T(8,128)S(1)} %get-tuple-element.6), channel_id=1, source_target_pairs={{0,10},{1,11},{2,12},{3,13},{4,14},{5,15},{6,16},{7,17},{8,18},{9,... | collective-permute-start | bytes 73736
  746.9 15.6 %collective-permute-start.16 = (f32[24,256]{1,0:T(8,128)S(1)}, f32[24,256]{1,0:T(8,128)S(1)}, u32[]{:S(2)}, u32[]{:S(2)}) collective-permute-start(f32[24,256]{1,0:T(8,128)S(1)} %get-tuple-element.6), channel_id=1, source_target_pairs={{0,11},{1,12},{2,13},{3,14},{4,15},{5,16},{6,17},{7,18},{8,19},{9,... | collective-permute-start | bytes 73736
  748.9 14.9 %collective-permute-start.17 = (f32[24,256]{1,0:T(8,128)S(1)}, f32[24,256]{1,0:T(8,128)S(1)}, u32[]{:S(2)}, u32[]{:S(2)}) collective-permute-start(f32[24,256]{1,0:T(8,128)S(1)} %get-tuple-element.6), channel_id=1, source_target_pairs={{0,12},{1,13},{2,14},{3,15},{4,16},{5,17},{6,18},{7,19},{8,20},{9,... | collective-permute-start | bytes 73736
  751.8 13.3 %collective-permute-start.18 = (f32[24,256]{1,0:T(8,128)S(1)}, f32[24,256]{1,0:T(8,128)S(1)}, u32[]{:S(2)}, u32[]{:S(2)}) collective-permute-start(f32[24,256]{1,0:T(8,128)S(1)} %get-tuple-element.6), channel_id=1, source_target_pairs={{0,13},{1,14},{2,15},{3,16},{4,17},{5,18},{6,19},{7,20},{8,21},{9,... | collective-permute-start | bytes 73736
  754.6 13.2 %collective-permute-start.19 = (f32[24,256]{1,0:T(8,128)S(1)}, f32[24,256]{1,0:T(8,128)S(1)}, u32[]{:S(2)}, u32[]{:S(2)}) collective-permute-start(f32[24,256]{1,0:T(8,128)S(1)} %get-tuple-element.6), channel_id=1, source_target_pairs={{0,14},{1,15},{2,16},{3,17},{4,18},{5,19},{6,20},{7,21},{8,22},{9,... | collective-permute-start | bytes 73736
  758.5 12.8 %collective-permute-start.20 = (f32[24,256]{1,0:T(8,128)S(1)}, f32[24,256]{1,0:T(8,128)S(1)}, u32[]{:S(2)}, u32[]{:S(2)}) collective-permute-start(f32[24,256]{1,0:T(8,128)S(1)} %get-tuple-element.6), channel_id=1, source_target_pairs={{0,15},{1,16},{2,17},{3,18},{4,19},{5,20},{6,21},{7,22},{8,23},{9,... | collective-permute-start | bytes 73736
  773.0 13.1 %collective-permute-start.26 = (f32[24,256]{1,0:T(8,128)S(1)}, f32[24,256]{1,0:T(8,128)S(1)}, u32[]{:S(2)}, u32[]{:S(2)}) collective-permute-start(f32[24,256]{1,0:T(8,128)S(1)} %get-tuple-element.6), channel_id=1, source_target_pairs={{0,21},{1,22},{2,23},{3,24},{4,25},{5,26},{6,27},{7,28},{8,29},{9,... | collective-permute-start | bytes 73736
  775.0 14.0 %collective-permute-start.27 = (f32[24,256]{1,0:T(8,128)S(1)}, f32[24,256]{1,0:T(8,128)S(1)}, u32[]{:S(2)}, u32[]{:S(2)}) collective-permute-start(f32[24,256]{1,0:T(8,128)S(1)} %get-tuple-element.6), channel_id=1, source_target_pairs={{0,22},{1,23},{2,24},{3,25},{4,26},{5,27},{6,28},{7,29},{8,30},{9,... | collective-permute-start | bytes 73736
  777.0 13.6 %collective-permute-start.28 = (f32[24,256]{1,0:T(8,128)S(1)}, f32[24,256]{1,0:T(8,128)S(1)}, u32[]{:S(2)}, u32[]{:S(2)}) collective-permute-start(f32[24,256]{1,0:T(8,128)S(1)} %get-tuple-element.6), channel_id=1, source_target_pairs={{0,23},{1,24},{2,25},{3,26},{4,27},{5,28},{6,29},{7,30},{8,31},{9,... | collective-permute-start | bytes 73736
  778.5 14.2 %collective-permute-start.29 = (f32[24,256]{1,0:T(8,128)S(1)}, f32[24,256]{1,0:T(8,128)S(1)}, u32[]{:S(2)}, u32[]{:S(2)}) collective-permute-start(f32[24,256]{1,0:T(8,128)S(1)} %get-tuple-element.6), channel_id=1, source_target_pairs={{0,24},{1,25},{2,26},{3,27},{4,28},{5,29},{6,30},{7,31},{8,32},{9,... | collective-permute-start | bytes 73736
  780.8 13.1 %collective-permute-start.30 = (f32[24,256]{1,0:T(8,128)S(1)}, f32[24,256]{1,0:T(8,128)S(1)}, u32[]{:S(2)}, u32[]{:S(2)}) collective-permute-start(f32[24,256]{1,0:T(8,128)S(1)} %get-tuple-element.6), channel_id=1, source_target_pairs={{0,25},{1,26},{2,27},{3,28},{4,29},{5,30},{6,31},{7,32},{8,33},{9,... | collective-permute-start | bytes 73736
  786.2 17.4 %collective-permute-start.31 = (f32[24,256]{1,0:T(8,128)S(1)}, f32[24,256]{1,0:T(8,128)S(1)}, u32[]{:S(2)}, u32[]{:S(2)}) collective-permute-start(f32[24,256]{1,0:T(8,128)S(1)} %get-tuple-element.6), channel_id=1, source_target_pairs={{0,26},{1,27},{2,28},{3,29},{4,30},{5,31},{6,32},{7,33},{8,34},{9,... | collective-permute-start | bytes 73736
  789.0 15.9 %collective-permute-start.32 = (f32[24,256]{1,0:T(8,128)S(1)}, f32[24,256]{1,0:T(8,128)S(1)}, u32[]{:S(2)}, u32[]{:S(2)}) collective-permute-start(f32[24,256]{1,0:T(8,128)S(1)} %get-tuple-element.6), channel_id=1, source_target_pairs={{0,27},{1,28},{2,29},{3,30},{4,31},{5,32},{6,33},{7,34},{8,35},{9,... | collective-permute-start | bytes 73736
  790.6 16.2 %collective-permute-start.33 = (f32[24,256]{1,0:T(8,128)S(1)}, f32[24,256]{1,0:T(8,128)S(1)}, u32[]{:S(2)}, u32[]{:S(2)}) collective-permute-start(f32[24,256]{1,0:T(8,128)S(1)} %get-tuple-element.6), channel_id=1, source_target_pairs={{0,28},{1,29},{2,30},{3,31},{4,32},{5,33},{6,34},{7,35},{8,36},{9,... | collective-permute-start | bytes 73736
  792.6 17.0 %collective-permute-start.34 = (f32[24,256]{1,0:T(8,128)S(1)}, f32[24,256]{1,0:T(8,128)S(1)}, u32[]{:S(2)}, u32[]{:S(2)}) collective-permute-start(f32[24,256]{1,0:T(8,128)S(1)} %get-tuple-element.6), channel_id=1, source_target_pairs={{0,29},{1,30},{2,31},{3,32},{4,33},{5,34},{6,35},{7,36},{8,37},{9,... | collective-permute-start | bytes 73736
  793.9 20.1 %collective-permute-start.35 = (f32[24,256]{1,0:T(8,128)S(1)}, f32[24,256]{1,0:T(8,128)S(1)}, u32[]{:S(2)}, u32[]{:S(2)}) collective-permute-start(f32[24,256]{1,0:T(8,128)S(1)} %get-tuple-element.6), channel_id=1, source_target_pairs={{0,30},{1,31},{2,32},{3,33},{4,34},{5,35},{6,36},{7,37},{8,38},{9,... | collective-permute-start | bytes 73736
  803.6 13.0 %collective-permute-start.36 = (f32[24,256]{1,0:T(8,128)S(1)}, f32[24,256]{1,0:T(8,128)S(1)}, u32[]{:S(2)}, u32[]{:S(2)}) collective-permute-start(f32[24,256]{1,0:T(8,128)S(1)} %get-tuple-element.6), channel_id=1, source_target_pairs={{0,31},{1,32},{2,33},{3,34},{4,35},{5,36},{6,37},{7,38},{8,39},{9,... | collective-permute-start | bytes 73736
  (98 other events, 1129.9 us)
Sparse Core Ops, SparseCore 0:
  9.7 209.9 all-gather.2
